TPU v7x, 512 devices: a whole 4x8x8 slice. The times are simulated.
512 devices in a mesh: section: 2 (over core), sy: 8 (over y), sx: 8 (over z), mb: 4 (over x).
Axes of the slice: x: 4, y: 8, z: 8, core: 2. Of those that a mesh axis runs over, the one named last changes fastest.
Arguments:
- frames: bfloat16 [4, 512, 512, 128], P('mb', 'sy', 'sx'), may hold values from -6 to 6
- encode_weight: bfloat16 [512, 384], replicated, may hold values from -0.25 to 0.25
- conv_weight: bfloat16 [2, 1, 3456, 384], P('section', None, ('sy', 'sx')), may hold values from -0.109375 to 0.109375
- norm_gain: float32 [2, 1, 384], P('section'), may hold values from 0.1 to 1.9
- head_weight: bfloat16 [384, 256], replicated, may hold values from -0.3125 to 0.3125
- prior_logits: bfloat16 [4, 256, 256, 256], P('mb', 'sy', 'sx'), may hold values from -12 to 249
- target_bins: int32 [4, 256, 256], P('mb', 'sy', 'sx'), may hold values from 0 to 255
Outputs:
- section_features: bfloat16 [2, 4, 256, 256, 384], P('section', 'mb', 'sy', 'sx')
- head_step: float32 [384, 256], P('section')
- mean_loss: float32 [], replicated
All inputs are finite; a program needn't handle non-finite values.
Results may differ from a plain program's by a relative error of at most 0.008.
Values may be sent and summed in bfloat16 or wider, within the bound.
No kernel may reach another device: no remote copies, remote signals or barrier semaphores. Data moves between devices by JAX's collectives and lax.ppermute only.
A program may use at most 64 MiB of HBM per device.

v0:
```python
import jax
import jax.numpy as jnp
from jax import lax
from jax.sharding import PartitionSpec as P

FIRST_DILATION = 1
SECTION_FACTOR = 8


def norm_gelu(activations, gain):
    values = activations.astype(jnp.float32)
    center = jnp.mean(values, axis=-1, keepdims=True)
    offset = values - center
    spread = jnp.mean(offset * offset, axis=-1, keepdims=True)
    normed = offset * lax.rsqrt(spread + 1e-05) * gain
    return jax.nn.gelu(normed, approximate=False).astype(jnp.bfloat16)


def copies_to(block, axes, count):
    return lax.all_to_all(
        jnp.broadcast_to(block[None], (count,) + block.shape),
        axes,
        split_axis=0,
        concat_axis=0,
        tiled=True,
    )


def swap(block):
    return lax.ppermute(block, "section", [(0, 1), (1, 0)])


def patches_of(padded, rows, columns, step):
    channels = padded.shape[-1]
    windows = [
        padded[i * step : i * step + rows, j * step : j * step + columns]
        for i in range(3)
        for j in range(3)
    ]
    return jnp.concatenate(windows, axis=2).reshape(rows * columns, 9 * channels)


def split_two(value):
    high = value.astype(jnp.bfloat16)
    low = (value - high.astype(jnp.float32)).astype(jnp.bfloat16)
    return (high, low)


def per_device(
    frames, encode_weight, conv_weight, norm_gain, head_weight, prior_logits, target_bins
):
    section = lax.axis_index("section")
    first = section == 0
    parts_y = lax.axis_size("sy")
    parts_x = lax.axis_size("sx")
    parts_b = lax.axis_size("mb")
    side = frames.shape[1] // 2
    half = side // 2
    channels = encode_weight.shape[1]
    bins = head_weight.shape[1]
    near = FIRST_DILATION
    far = FIRST_DILATION * SECTION_FACTOR
    reach = near + far
    shard = conv_weight[0, 0]
    strip = copies_to(shard, "sx", parts_x).reshape(parts_x * shard.shape[0], channels)
    weight_own = lax.all_gather(strip, "sy", axis=0, tiled=True)
    gain_own = norm_gain[0, 0]
    gain_other = swap(gain_own)
    gain_0 = jnp.where(first, gain_own, gain_other)
    gain_1 = jnp.where(first, gain_other, gain_own)
    blocks = frames[0].reshape(side, 2, side, 2, frames.shape[3])
    kernel = encode_weight.reshape(2, 2, frames.shape[3], channels)
    encoded = jnp.einsum(
        "apbqc,pqco->abo", blocks, kernel, preferred_element_type=jnp.float32
    ).astype(jnp.bfloat16)
    outgoing = jnp.where(first, encoded[side - reach :], encoded[:reach])
    route = [(y, y + 1) for y in range(parts_y - 1)] + [
        (parts_y + y + 1, parts_y + y) for y in range(parts_y - 1)
    ]
    arrived = lax.ppermute(outgoing, ("section", "sy"), route)
    rows = jnp.where(
        first,
        jnp.concatenate([arrived, encoded[: half + reach]], axis=0),
        jnp.concatenate([encoded[half - reach :], arrived], axis=0),
    )
    forward = [(x, x + 1) for x in range(parts_x - 1)]
    backward = [(x + 1, x) for x in range(parts_x - 1)]
    left = lax.ppermute(rows[:, side - reach :], "sx", forward)
    right = lax.ppermute(rows[:, :reach], "sx", backward)
    haloed = jnp.concatenate([left, rows, right], axis=1)
    tall, wide = (half + 2 * far, side + 2 * far)
    hidden = norm_gelu(haloed, gain_0)
    patches = patches_of(hidden, tall, wide, near)
    weight_own, patches = lax.optimization_barrier((weight_own, patches))
    weight_other = swap(weight_own)
    weight_0 = jnp.where(first, weight_own, weight_other)
    weight_1 = jnp.where(first, weight_other, weight_own)
    summed = jnp.dot(patches, weight_0, preferred_element_type=jnp.float32)
    features_0 = (
        haloed[near : near + tall, near : near + wide].astype(jnp.float32)
        + summed.reshape(tall, wide, channels)
    ).astype(jnp.bfloat16)
    row_at = (
        lax.axis_index("sy") * side
        + section * half
        - far
        + lax.broadcasted_iota(jnp.int32, (tall, wide, 1), 0)
    )
    column_at = (
        lax.axis_index("sx") * side - far + lax.broadcasted_iota(jnp.int32, (tall, wide, 1), 1)
    )
    inside = (
        (row_at >= 0) & (row_at < side * parts_y) & (column_at >= 0) & (column_at < side * parts_x)
    )
    hidden = jnp.where(inside, norm_gelu(features_0, gain_1), jnp.bfloat16(0))
    patches = patches_of(hidden, half, side, far)
    summed = jnp.dot(patches, weight_1, preferred_element_type=jnp.float32)
    own_0 = features_0[far : far + half, far : far + side]
    own_1 = (own_0.astype(jnp.float32) + summed.reshape(half, side, channels)).astype(jnp.bfloat16)
    cells = half * side
    flat = own_1.reshape(cells, channels)
    prior = lax.dynamic_slice_in_dim(prior_logits[0], section * half, half, axis=0)
    target = lax.dynamic_slice_in_dim(target_bins[0], section * half, half, axis=0)
    logits = jnp.dot(flat, head_weight, preferred_element_type=jnp.float32)
    logits = logits + prior.reshape(cells, bins).astype(jnp.float32)
    row_top = jnp.max(logits, axis=1, keepdims=True)
    shifted = logits - row_top
    exp_terms = jnp.exp(shifted)
    exp_total = jnp.sum(exp_terms, axis=1, keepdims=True)
    softmax_rows = exp_terms / exp_total
    onehot = (target.reshape(cells, 1) == lax.broadcasted_iota(jnp.int32, (1, bins), 1)).astype(
        jnp.float32
    )
    loss_sum = jnp.sum(jnp.log(exp_total[:, 0]) - jnp.sum(shifted * onehot, axis=1))
    delta_rows = (softmax_rows - onehot).astype(jnp.bfloat16)
    gradient = lax.dot_general(
        flat, delta_rows, (((0,), (0,)), ((), ())), preferred_element_type=jnp.float32
    )
    slots = parts_x * parts_b
    slot_rows = channels // slots

    def with_loss(values, loss):
        high, low = split_two(loss)
        lane = lax.broadcasted_iota(jnp.int32, (1, bins), 1)
        row = jnp.where(lane == 0, high, jnp.where(lane == 1, low, jnp.bfloat16(0)))
        row = jnp.broadcast_to(row, values.shape[:-2] + (1, bins))
        return jnp.concatenate([values.astype(jnp.bfloat16), row], axis=-2)

    packed = with_loss(gradient.reshape(slots, slot_rows, bins), loss_sum)
    packed = lax.all_to_all(packed, ("sx", "mb"), split_axis=0, concat_axis=0, tiled=True)
    partial = jnp.sum(packed.astype(jnp.float32), axis=0)
    packed = with_loss(partial[:slot_rows], partial[slot_rows, 0] + partial[slot_rows, 1])
    packed = copies_to(packed, ("section", "sy"), 2 * parts_y)
    partial = jnp.sum(packed.astype(jnp.float32), axis=0)
    loss_all = partial[slot_rows, 0] + partial[slot_rows, 1]
    gathered = copies_to(partial[:slot_rows].astype(jnp.bfloat16), ("sx", "mb"), slots)
    gradient = gathered.reshape(channels, bins).astype(jnp.float32)
    scale = lax.rsqrt(jnp.mean(gradient * gradient) + 1e-06)
    own_rows = lax.dynamic_slice_in_dim(gradient, section * (channels // 2), channels // 2, axis=0)
    head_step = own_rows * scale
    mean_loss = loss_all / (parts_b * parts_y * parts_x * side * side)
    sent = swap(jnp.where(first, own_1, own_0))
    stacked = jnp.where(
        first, jnp.concatenate([own_0, sent], axis=0), jnp.concatenate([sent, own_1], axis=0)
    )[None, None]
    return (stacked, head_step, mean_loss)


def solution(mesh):
    placed = (
        P("mb", "sy", "sx", None),
        P(),
        P("section", None, ("sy", "sx"), None),
        P("section", None, None),
        P(),
        P("mb", "sy", "sx", None),
        P("mb", "sy", "sx"),
    )
    return jax.shard_map(
        per_device,
        mesh=mesh,
        in_specs=placed,
        out_specs=(P("section", "mb", "sy", "sx", None), P("section", None), P()),
        check_vma=False,
    )
```

profile of v0, /device:TPU:8, one launch (start us, length us, event | category | flops | bytes accessed | tf_op | source)
XLA Modules:
  0.0 193.8 jit_solution(5893310341925343398)
XLA Ops:
  7.2 2.1 %bitcast_convert_fusion = bf16[32,32,384]{2,1,0:T(8,128)(2,1)S(1)} fusion(bf16[2,2,128,384,1]{3,2,1,0,4:T(8,128)(2,1)} %bitcast.43, bf16[32,2,32,2,128]{4,3,2,1,0:T(2,128)(2,1)} %bitcast.42), kind=kOutput, calls=%fused_computation.66 | convolution fusion | flops 403046400 | bytes 2228224 | tf_op jit(solution)/shard_map/apbqc,pqco->abo/dot_general | solution.py:73
  9.3 3.6 %collective-permute-start = (bf16[9,32,384]{2,1,0:T(8,128)(2,1)S(1)}, bf16[9,32,384]{2,1,0:T(8,128)(2,1)S(1)}, u32[]{:S(2)}, u32[]{:S(2)}) collective-permute-start(bf16[9,32,384]{2,1,0:T(8,128)(2,1)S(1)} %slice_select_fusion), channel_id=1, source_target_pairs={{0,32},{32,64},{64,96},{96,128},{128,160},{160,192},{192,224},{288... | collective-permute-start | bytes 663560 | tf_op jit(solution)/shard_map/ppermute | solution.py:80
  13.1 7.4 %collective-permute-done = bf16[9,32,384]{2,1,0:T(8,128)(2,1)S(1)} collective-permute-done((bf16[9,32,384]{2,1,0:T(8,128)(2,1)S(1)}, bf16[9,32,384]{2,1,0:T(8,128)(2,1)S(1)}, u32[]{:S(2)}, u32[]{:S(2)}) %collective-permute-start) | collective-permute-done | bytes 221216 | tf_op jit(solution)/shard_map/ppermute | solution.py:80
  20.8 1.3 collective-permute-start.1
  22.1 1.3 collective-permute-start.2
  23.4 1.9 collective-permute-start.3
  26.1 11.6 %all-to-all-start = ((bf16[8,54,384]{2,1,0:T(8,128)(2,1)}), bf16[8,54,384]{2,1,0:T(8,128)(2,1)S(1)}, u32[]{:S(2)}, u32[]{:S(2)}) async-start(bf16[8,54,384]{2,1,0:T(8,128)(2,1)} %broadcast_in_dim.65), calls=%async_computation | async-start | bytes 688128 | tf_op jit(solution)/shard_map/all_to_all | solution.py:20
  38.5 1.7 convert_reduce_fusion
  41.1 10.9 %all-to-all-done = bf16[8,54,384]{2,1,0:T(8,128)(2,1)S(1)} async-done(((bf16[8,54,384]{2,1,0:T(8,128)(2,1)}), bf16[8,54,384]{2,1,0:T(8,128)(2,1)S(1)}, u32[]{:S(2)}, u32[]{:S(2)}) %all-to-all-start) | async-done | bytes 331808 | tf_op jit(solution)/shard_map/all_to_all | solution.py:20
  52.8 6.8 %fusion.7 = bf16[34,50,384]{2,1,0:T(8,128)(2,1)S(1)} fusion(bf16[34,50,384]{2,1,0:T(8,128)(2,1)S(1)} %get-tuple-element.14, f32[384]{0:T(512)S(1)} %get-tuple-element.25, f32[34,50]{1,0:T(8,128)S(1)} %add_rsqrt_fusion, f32[34,50]{1,0:T(8,128)S(1)} %broadcast_multiply_fusion), kind=kLoop, calls=%fused_computation.13 | loop fusion | flops 45043200 | bytes 2626336 | tf_op jit(solution)/shard_map/convert_element_type | solution.py:16
  59.6 1.2 slice_dynamic-update-slice_fusion.8
  60.8 1.6 slice_dynamic-update-slice_fusion.7
  62.4 1.6 slice_dynamic-update-slice_fusion.6
  64.1 1.2 slice_dynamic-update-slice_fusion.5
  65.2 1.6 slice_dynamic-update-slice_fusion.4
  66.9 1.6 slice_dynamic-update-slice_fusion.3
  68.5 1.2 slice_dynamic-update-slice_fusion.2
  69.7 1.6 slice_dynamic-update-slice_fusion.1
  71.3 1.6 slice_dynamic-update-slice_fusion
  72.9 22.1 %all-gather.2.cloned.1.call-done = bf16[3456,384]{1,0:T(8,128)(2,1)} async-done(((bf16[432,384]{1,0:T(8,128)(2,1)}), bf16[3456,384]{1,0:T(8,128)(2,1)}) %all-gather.2.cloned.1.call-update) | async-done | bytes 2654224 | tf_op jit(solution)/shard_map/all_gather | solution.py:66
  95.0 2.1 %collective-permute-start.4 = (bf16[3456,384]{1,0:T(8,128)(2,1)}, bf16[3456,384]{1,0:T(8,128)(2,1)}, u32[]{:S(2)}, u32[]{:S(2)}) collective-permute-start(bf16[3456,384]{1,0:T(8,128)(2,1)} %all-gather.2.cloned.1.call-done), channel_id=1, source_target_pairs={{0,256},{256,0},{1,257},{257,1},{2,258},{258,2},{3,259},{259,3},{4... | collective-permute-start | bytes 7962632 | tf_op jit(solution)/shard_map/ppermute | solution.py:30
  97.6 4.6 %collective-permute-done.4 = bf16[3456,384]{1,0:T(8,128)(2,1)} collective-permute-done((bf16[3456,384]{1,0:T(8,128)(2,1)}, bf16[3456,384]{1,0:T(8,128)(2,1)}, u32[]{:S(2)}, u32[]{:S(2)}) %collective-permute-start.4) | collective-permute-done | bytes 2654240 | tf_op jit(solution)/shard_map/ppermute | solution.py:30
  102.1 9.3 %fusion.25 = f32[1536,384]{1,0:T(8,128)S(1)} fusion(bf16[1536,3456]{1,0:T(8,128)(2,1)} %bitcast.6, bf16[3456,384]{1,0:T(8,128)(2,1)} %all-gather.2.cloned.1.call-done, bf16[3456,384]{1,0:T(8,128)(2,1)} %collective-permute-done.4, pred[]{:T(512)S(6)} %eq.50), kind=kOutput, calls=%fused_computation.37 | convolution fusion | flops 4078190592 | bytes 18284544 | tf_op jit(solution)/shard_map/dot_general | solution.py:98
  112.7 6.2 %fusion.47 = bf16[32,48,384]{2,1,0:T(8,128)(2,1)S(1)} fusion(bf16[32,48,384]{2,1,0:T(8,128)(2,1)S(1)} %get-tuple-element.12, f32[384]{0:T(512)S(1)} %get-tuple-element.24, f32[32,48]{1,0:T(8,128)S(1)} %add_rsqrt_fusion.1, f32[32,48]{1,0:T(8,128)S(1)} %broadcast_multiply_fusion.1, pred[32,48]{1,0:T(8,128)(4,1)S(1)} %and_and_fusion), kind=kLoop, calls=%fused_computation.69 | loop fusion | flops 41287680 | bytes 2374656 | tf_op jit(solution)/shard_map/jit(_where)/select_n | solution.py:115
  119.6 1.2 copy-done.6
  120.8 3.9 %broadcast_select_fusion = (bf16[16,32,384]{2,1,0:T(8,128)(2,1)S(1)}, bf16[16,32,384]{2,1,0:T(8,128)(2,1)S(1)}, bf16[1,1,16,32,384]{4,3,2,1,0:T(8,128)(2,1)S(1)}) fusion(pred[]{:T(512)S(6)} %eq.50, bf16[32,48,384]{2,1,0:T(8,128)(2,1)S(1)} %get-tuple-element.12, bf16[16,32,3456]{2,1,0:T(8,128)(2,1)S(1)} %slice_dynamic-update-slice_fusion.9, ...), kind=kOutput, calls=%fused_computation.100 | convolution fusion | flops 1361068032 | bytes 10421248 | tf_op jit(solution)/shard_map/dot_general | solution.py:117
  128.2 21.7 %all_to_all.20 = bf16[32,13,256]{2,1,0:T(8,128)(2,1)S(1)} all-to-all(bf16[32,13,256]{2,1,0:T(8,128)(2,1)S(1)} %copy.42), channel_id=1, replica_groups=mesh['section'=2,'sy'=8,'sx'=8,'mb'=4] {'sx','mb'}, dimensions={0} | all-to-all | bytes 425984 | tf_op jit(solution)/shard_map/all_to_all | solution.py:150
  152.5 5.3 %all-to-all-start.2 = ((bf16[16,13,256]{2,1,0:T(8,128)(2,1)}), bf16[16,13,256]{2,1,0:T(8,128)(2,1)S(1)}, u32[]{:S(2)}, u32[]{:S(2)}) async-start(bf16[16,13,256]{2,1,0:T(8,128)(2,1)} %broadcast_in_dim.75), calls=%async_computation.2 | async-start | bytes 262144 | tf_op jit(solution)/shard_map/all_to_all | solution.py:20
  157.8 2.0 %collective-permute-start.5 = (bf16[16,32,384]{2,1,0:T(8,128)(2,1)S(1)}, bf16[16,32,384]{2,1,0:T(8,128)(2,1)S(1)}, u32[]{:S(2)}, u32[]{:S(2)}) collective-permute-start(bf16[16,32,384]{2,1,0:T(8,128)(2,1)S(1)} %get-tuple-element.9), channel_id=1, source_target_pairs={{0,256},{256,0},{1,257},{257,1},{2,258},{258,2},{3,259},{259,3},{4... | collective-permute-start | bytes 1179656 | tf_op jit(solution)/shard_map/ppermute | solution.py:30
  159.9 6.2 %all-to-all-done.2 = bf16[16,13,256]{2,1,0:T(8,128)(2,1)S(1)} async-done(((bf16[16,13,256]{2,1,0:T(8,128)(2,1)}), bf16[16,13,256]{2,1,0:T(8,128)(2,1)S(1)}, u32[]{:S(2)}, u32[]{:S(2)}) %all-to-all-start.2) | async-done | bytes 106528 | tf_op jit(solution)/shard_map/all_to_all | solution.py:20
  166.8 3.9 %all-to-all-start.3 = ((bf16[32,12,256]{2,1,0:T(8,128)(2,1)}), bf16[32,12,256]{2,1,0:T(8,128)(2,1)S(1)}, u32[]{:S(2)}, u32[]{:S(2)}) async-start(bf16[32,12,256]{2,1,0:T(8,128)(2,1)} %broadcast_in_dim.76), calls=%async_computation.3 | async-start | bytes 524288 | tf_op jit(solution)/shard_map/all_to_all | solution.py:20
  173.6 10.0 %all-to-all-done.3 = bf16[32,12,256]{2,1,0:T(8,128)(2,1)S(1)} async-done(((bf16[32,12,256]{2,1,0:T(8,128)(2,1)}), bf16[32,12,256]{2,1,0:T(8,128)(2,1)S(1)}, u32[]{:S(2)}, u32[]{:S(2)}) %all-to-all-start.3) | async-done | bytes 196640 | tf_op jit(solution)/shard_map/all_to_all | solution.py:20
  (75 shorter events, 13.3 us)
Async XLA Ops:
  7.2 89.9 %copy-start = (bf16[1,32,32,256]{3,2,1,0:T(8,128)(2,1)S(1)}, bf16[1,32,32,256]{3,2,1,0:T(8,128)(2,1)}, u32[]{:S(2)}) copy-start(bf16[1,32,32,256]{3,2,1,0:T(8,128)(2,1)} %param.12) | copy-start | bytes 1572868
  9.3 14.1 %copy-start.5 = (f32[1,1,384]{2,1,0:T(1,128)S(1)}, f32[1,1,384]{2,1,0:T(1,128)}, u32[]{:S(2)}) copy-start(f32[1,1,384]{2,1,0:T(1,128)} %param.10) | copy-start | bytes 4612
  9.3 16.0 %copy-start.3 = (bf16[1,1,54,384]{3,2,1,0:T(8,128)(2,1)S(1)}, bf16[1,1,54,384]{3,2,1,0:T(8,128)(2,1)}, u32[]{:S(2)}) copy-start(bf16[1,1,54,384]{3,2,1,0:T(8,128)(2,1)} %param.9) | copy-start | bytes 124420
  9.3 11.1 %collective-permute-start = (bf16[9,32,384]{2,1,0:T(8,128)(2,1)S(1)}, bf16[9,32,384]{2,1,0:T(8,128)(2,1)S(1)}, u32[]{:S(2)}, u32[]{:S(2)}) collective-permute-start(bf16[9,32,384]{2,1,0:T(8,128)(2,1)S(1)} %slice_select_fusion), channel_id=1, source_target_pairs={{0,32},{32,64},{64,96},{96,128},{128,160},{160,192},{192,224},{288... | collective-permute-start | bytes 663560 | tf_op jit(solution)/shard_map/ppermute | solution.py:80
  20.8 17.0 %collective-permute-start.1 = (bf16[34,9,384]{2,1,0:T(8,128)(2,1)S(1)}, bf16[34,9,384]{2,1,0:T(8,128)(2,1)S(1)}, u32[]{:S(2)}, u32[]{:S(2)}) collective-permute-start(bf16[34,9,384]{2,1,0:T(8,128)(2,1)S(1)} %get-tuple-element.16), channel_id=1, source_target_pairs={{0,4},{4,8},{8,12},{12,16},{16,20},{20,24},{24,28},{1,5},{5,9},{9,... | collective-permute-start | bytes 705032 | tf_op jit(solution)/shard_map/ppermute | solution.py:88
  22.1 16.4 %collective-permute-start.2 = (bf16[34,9,384]{2,1,0:T(8,128)(2,1)S(1)}, bf16[34,9,384]{2,1,0:T(8,128)(2,1)}, u32[]{:S(2)}, u32[]{:S(2)}) collective-permute-start(bf16[34,9,384]{2,1,0:T(8,128)(2,1)S(1)} %get-tuple-element.17), channel_id=1, source_target_pairs={{4,0},{8,4},{12,8},{16,12},{20,16},{24,20},{28,24},{5,1},{9,5},{13... | collective-permute-start | bytes 705032 | tf_op jit(solution)/shard_map/ppermute | solution.py:89
  23.4 14.3 %collective-permute-start.3 = (f32[384]{0:T(512)S(1)}, f32[384]{0:T(512)S(1)}, u32[]{:S(2)}, u32[]{:S(2)}) collective-permute-start(f32[384]{0:T(512)S(1)} %reduce.1), channel_id=1, source_target_pairs={{0,256},{256,0},{1,257},{257,1},{2,258},{258,2},{3,259},{259,3},{4... | collective-permute-start | bytes 4616 | tf_op jit(solution)/shard_map/ppermute | solution.py:30
  26.1 25.8 %all-to-all-start = ((bf16[8,54,384]{2,1,0:T(8,128)(2,1)}), bf16[8,54,384]{2,1,0:T(8,128)(2,1)S(1)}, u32[]{:S(2)}, u32[]{:S(2)}) async-start(bf16[8,54,384]{2,1,0:T(8,128)(2,1)} %broadcast_in_dim.65), calls=%async_computation | async-start | bytes 688128 | tf_op jit(solution)/shard_map/all_to_all | solution.py:20
  37.7 57.3 %all-gather.2.cloned.1.call-start = ((), (), s32[]{:S(2)}) async-start(), calls=%async_computation.4 | async-start | bytes 2985984 | tf_op jit(solution)/shard_map/all_gather | solution.py:66
  37.8 0.8 copy-start.1
  71.3 26.1 %copy-start.4 = (s32[1,32,32]{2,1,0:T(8,128)S(1)}, s32[1,32,32]{2,1,0:T(8,128)}, u32[]{:S(2)}) copy-start(s32[1,32,32]{2,1,0:T(8,128)} %param.13) | copy-start | bytes 12292
  95.0 7.2 %collective-permute-start.4 = (bf16[3456,384]{1,0:T(8,128)(2,1)}, bf16[3456,384]{1,0:T(8,128)(2,1)}, u32[]{:S(2)}, u32[]{:S(2)}) collective-permute-start(bf16[3456,384]{1,0:T(8,128)(2,1)} %all-gather.2.cloned.1.call-done), channel_id=1, source_target_pairs={{0,256},{256,0},{1,257},{257,1},{2,258},{258,2},{3,259},{259,3},{4... | collective-permute-start | bytes 7962632 | tf_op jit(solution)/shard_map/ppermute | solution.py:30
  119.1 1.8 copy-start.6
  120.8 4.2 %copy-start.2 = (bf16[384,256]{1,0:T(8,128)(2,1)S(1)}, bf16[384,256]{1,0:T(8,128)(2,1)}, u32[]{:S(2)}) copy-start(bf16[384,256]{1,0:T(8,128)(2,1)} %param.11) | copy-start | bytes 589828
  152.5 13.5 %all-to-all-start.2 = ((bf16[16,13,256]{2,1,0:T(8,128)(2,1)}), bf16[16,13,256]{2,1,0:T(8,128)(2,1)S(1)}, u32[]{:S(2)}, u32[]{:S(2)}) async-start(bf16[16,13,256]{2,1,0:T(8,128)(2,1)} %broadcast_in_dim.75), calls=%async_computation.2 | async-start | bytes 262144 | tf_op jit(solution)/shard_map/all_to_all | solution.py:20
  157.8 12.9 %collective-permute-start.5 = (bf16[16,32,384]{2,1,0:T(8,128)(2,1)S(1)}, bf16[16,32,384]{2,1,0:T(8,128)(2,1)S(1)}, u32[]{:S(2)}, u32[]{:S(2)}) collective-permute-start(bf16[16,32,384]{2,1,0:T(8,128)(2,1)S(1)} %get-tuple-element.9), channel_id=1, source_target_pairs={{0,256},{256,0},{1,257},{257,1},{2,258},{258,2},{3,259},{259,3},{4... | collective-permute-start | bytes 1179656 | tf_op jit(solution)/shard_map/ppermute | solution.py:30
  166.8 16.8 %all-to-all-start.3 = ((bf16[32,12,256]{2,1,0:T(8,128)(2,1)}), bf16[32,12,256]{2,1,0:T(8,128)(2,1)S(1)}, u32[]{:S(2)}, u32[]{:S(2)}) async-start(bf16[32,12,256]{2,1,0:T(8,128)(2,1)} %broadcast_in_dim.76), calls=%async_computation.3 | async-start | bytes 524288 | tf_op jit(solution)/shard_map/all_to_all | solution.py:20
Sparse Core Ops, SparseCore 0:
  52.9 41.9 all-gather.1
where the time goes:
time: 195 us; the launch traced here: 194 us
  waiting for transfers between devices  61 us (31%)
  starting transfers between devices  33 us (17%)
  blocking collectives  21.7 us (11%)
  local copies, waits for them, and re-layouts  21 us (11%)
  other arithmetic  20.7 us (11%)
  between operations  20.3 us (10%)
  matrix products  16.1 us (8%)
    all_to_all x3, waiting for transfers between devices, copies_to(): lax.all_to_all(jnp.broadcast_to(block[None], (count,) + block.shape), axe...  27 us
    all_gather x1, waiting for transfers between devices, per_device(): weight_own = lax.all_gather(strip, 'sy', axis=0, tiled=True)  22.1 us
    all_to_all x1, blocking collectives, per_device(): lax.all_to_all(packed, ('sx', 'mb'), split_axis=0, concat_axis=0, tiled=T...  21.7 us
    all_to_all x3, starting transfers between devices, copies_to(): lax.all_to_all(jnp.broadcast_to(block[None], (count,) + block.shape), axe...  20.7 us
    unnamed x30, local copies, waits for them, and re-layouts  14.2 us
    dot_general x1, matrix products, per_device(): summed = jnp.dot(patches, weight_0, preferred_element_type=jnp.float32)  9.26 us
    ppermute x1, waiting for transfers between devices, per_device(): arrived = lax.ppermute(outgoing, ('section', 'sy'), route)  7.39 us
    convert_element_type x1, other arithmetic, norm_gelu(): return jax.nn.gelu(normed, approximate=False).astype(jnp.bfloat16)  6.79 us
  transfers between devices with their start and end apart: 10, of which 6 were waited for; matrix products, arithmetic and copies ran while one was open for 14% of the time, Pallas kernels for 0%

commit v1 on v0

--- a/solution.py
+++ b/solution.py
@@ -63,7 +63,8 @@
     reach = near + far
     shard = conv_weight[0, 0]
     strip = copies_to(shard, "sx", parts_x).reshape(parts_x * shard.shape[0], channels)
-    weight_own = lax.all_gather(strip, "sy", axis=0, tiled=True)
+    repeated = jnp.stack([strip] * lax.axis_size("sy"))
+    weight_own = jnp.concatenate(lax.all_to_all(repeated, "sy", 0, 0), axis=0)
     gain_own = norm_gain[0, 0]
     gain_other = swap(gain_own)
     gain_0 = jnp.where(first, gain_own, gain_other)

time: 195 us -> 205 us (1.051)
  waiting for transfers between devices: 61 us -> 81 us
  between operations: 20.3 us -> 6.87 us
  starting transfers between devices: 33 us -> 41.3 us
  blocking collectives: 21.7 us -> 17.7 us
    all_to_all x0 -> x1, waiting for transfers between devices: none -> 41.9 us  [per_device(): weight_own = jnp.concatenate(lax.all_to_all(repeated, 'sy', 0, 0), axis=0)]
    all_gather x1 -> x0, waiting for transfers between devices: 22.1 us -> none  [per_device(): weight_own = lax.all_gather(strip, 'sy', axis=0, tiled=True)]
    all_to_all x0 -> x1, starting transfers between devices: none -> 8.75 us  [per_device(): weight_own = jnp.concatenate(lax.all_to_all(repeated, 'sy', 0, 0), axis=0)]
    all_to_all x1, blocking collectives: 21.7 us -> 17.7 us  [per_device(): lax.all_to_all(packed, ('sx', 'mb'), split_axis=0, concat_axis=0, tiled=T...]
    unnamed x30 -> x28, local copies, waits for them, and re-layouts: 14.2 us -> 13 us
  transfers between devices with their start and end apart: 10 -> 10, of which waited for: 6 -> 6; matrix products, arithmetic and copies ran while one was open for 14% -> 13% of each run, Pallas kernels for 0% -> 0%
where the time goes in v1:
time: 205 us; the launch traced here: 204 us
  waiting for transfers between devices  81 us (40%)
  starting transfers between devices  41.3 us (20%)
  local copies, waits for them, and re-layouts  20.7 us (10%)
  other arithmetic  20.7 us (10%)
  blocking collectives  17.7 us (9%)
  matrix products  16.1 us (8%)
  between operations  6.87 us (3%)
    all_to_all x1, waiting for transfers between devices, per_device(): weight_own = jnp.concatenate(lax.all_to_all(repeated, 'sy', 0, 0), axis=0)  41.9 us
    all_to_all x3, waiting for transfers between devices, copies_to(): lax.all_to_all(jnp.broadcast_to(block[None], (count,) + block.shape), axe...  27.1 us
    all_to_all x3, starting transfers between devices, copies_to(): lax.all_to_all(jnp.broadcast_to(block[None], (count,) + block.shape), axe...  20.3 us
    all_to_all x1, blocking collectives, per_device(): lax.all_to_all(packed, ('sx', 'mb'), split_axis=0, concat_axis=0, tiled=T...  17.7 us
    unnamed x28, local copies, waits for them, and re-layouts  13 us
    dot_general x1, matrix products, per_device(): summed = jnp.dot(patches, weight_0, preferred_element_type=jnp.float32)  9.26 us
    all_to_all x1, starting transfers between devices, per_device(): weight_own = jnp.concatenate(lax.all_to_all(repeated, 'sy', 0, 0), axis=0)  8.75 us
    ppermute x1, waiting for transfers between devices, per_device(): arrived = lax.ppermute(outgoing, ('section', 'sy'), route)  7.4 us
  transfers between devices with their start and end apart: 10, of which 6 were waited for; matrix products, arithmetic and copies ran while one was open for 13% of the time, Pallas kernels for 0%

profile of v1, /device:TPU:8, one launch (start us, length us, event | category | flops | bytes accessed | tf_op | source)
XLA Modules:
  0.0 204.3 jit_solution(6314150070524507794)
XLA Ops:
  0.7 2.1 %bitcast_convert_fusion = bf16[32,32,384]{2,1,0:T(8,128)(2,1)S(1)} fusion(bf16[2,2,128,384,1]{3,2,1,0,4:T(8,128)(2,1)} %bitcast.44, bf16[32,2,32,2,128]{4,3,2,1,0:T(2,128)(2,1)} %bitcast.43), kind=kOutput, calls=%fused_computation.66 | convolution fusion | flops 403046400 | bytes 2228224 | tf_op jit(solution)/shard_map/apbqc,pqco->abo/dot_general | solution.py:74
  2.8 3.6 %collective-permute-start = (bf16[9,32,384]{2,1,0:T(8,128)(2,1)S(1)}, bf16[9,32,384]{2,1,0:T(8,128)(2,1)S(1)}, u32[]{:S(2)}, u32[]{:S(2)}) collective-permute-start(bf16[9,32,384]{2,1,0:T(8,128)(2,1)S(1)} %slice_select_fusion), channel_id=1, source_target_pairs={{0,32},{32,64},{64,96},{96,128},{128,160},{160,192},{192,224},{288... | collective-permute-start | bytes 663560 | tf_op jit(solution)/shard_map/ppermute | solution.py:81
  6.5 7.4 %collective-permute-done = bf16[9,32,384]{2,1,0:T(8,128)(2,1)S(1)} collective-permute-done((bf16[9,32,384]{2,1,0:T(8,128)(2,1)S(1)}, bf16[9,32,384]{2,1,0:T(8,128)(2,1)S(1)}, u32[]{:S(2)}, u32[]{:S(2)}) %collective-permute-start) | collective-permute-done | bytes 221216 | tf_op jit(solution)/shard_map/ppermute | solution.py:81
  14.2 1.3 collective-permute-start.1
  15.6 1.3 collective-permute-start.2
  16.9 1.9 collective-permute-start.3
  19.6 11.5 %all-to-all-start = ((bf16[8,54,384]{2,1,0:T(8,128)(2,1)}), bf16[8,54,384]{2,1,0:T(8,128)(2,1)S(1)}, u32[]{:S(2)}, u32[]{:S(2)}) async-start(bf16[8,54,384]{2,1,0:T(8,128)(2,1)} %broadcast_in_dim.65), calls=%async_computation | async-start | bytes 688128 | tf_op jit(solution)/shard_map/all_to_all | solution.py:20
  31.9 1.7 convert_reduce_fusion
  34.5 10.9 %all-to-all-done = bf16[8,54,384]{2,1,0:T(8,128)(2,1)S(1)} async-done(((bf16[8,54,384]{2,1,0:T(8,128)(2,1)}), bf16[8,54,384]{2,1,0:T(8,128)(2,1)S(1)}, u32[]{:S(2)}, u32[]{:S(2)}) %all-to-all-start) | async-done | bytes 331808 | tf_op jit(solution)/shard_map/all_to_all | solution.py:20
  45.5 1.7 stack.3
  47.2 8.8 %all-to-all-start.1 = ((bf16[8,432,384]{2,1,0:T(8,128)(2,1)}), bf16[8,432,384]{2,1,0:T(8,128)(2,1)}, u32[]{:S(2)}, u32[]{:S(2)}) async-start(bf16[8,432,384]{2,1,0:T(8,128)(2,1)} %stack.3), calls=%async_computation.1 | async-start | bytes 5308416 | tf_op jit(solution)/shard_map/all_to_all | solution.py:67
  56.0 6.8 %fusion.7 = bf16[34,50,384]{2,1,0:T(8,128)(2,1)S(1)} fusion(bf16[34,50,384]{2,1,0:T(8,128)(2,1)S(1)} %get-tuple-element.14, f32[384]{0:T(512)S(1)} %get-tuple-element.25, f32[34,50]{1,0:T(8,128)S(1)} %add_rsqrt_fusion, f32[34,50]{1,0:T(8,128)S(1)} %broadcast_multiply_fusion), kind=kLoop, calls=%fused_computation.13 | loop fusion | flops 45043200 | bytes 2626336 | tf_op jit(solution)/shard_map/convert_element_type | solution.py:16
  62.8 1.2 slice_dynamic-update-slice_fusion.8
  64.0 1.6 slice_dynamic-update-slice_fusion.7
  65.6 1.6 slice_dynamic-update-slice_fusion.6
  68.4 1.6 slice_dynamic-update-slice_fusion.4
  70.0 1.6 slice_dynamic-update-slice_fusion.3
  71.7 1.2 slice_dynamic-update-slice_fusion.2
  72.9 1.6 slice_dynamic-update-slice_fusion.1
  74.5 1.6 slice_dynamic-update-slice_fusion
  76.1 41.9 %all-to-all-done.1 = bf16[8,432,384]{2,1,0:T(8,128)(2,1)} async-done(((bf16[8,432,384]{2,1,0:T(8,128)(2,1)}), bf16[8,432,384]{2,1,0:T(8,128)(2,1)}, u32[]{:S(2)}, u32[]{:S(2)}) %all-to-all-start.1) | async-done | bytes 2654240 | tf_op jit(solution)/shard_map/all_to_all | solution.py:67
  118.0 2.1 %collective-permute-start.4 = (bf16[3456,384]{1,0:T(8,128)(2,1)}, bf16[3456,384]{1,0:T(8,128)(2,1)}, u32[]{:S(2)}, u32[]{:S(2)}) collective-permute-start(bf16[3456,384]{1,0:T(8,128)(2,1)} %bitcast.6), channel_id=1, source_target_pairs={{0,256},{256,0},{1,257},{257,1},{2,258},{258,2},{3,259},{259,3},{4... | collective-permute-start | bytes 7962632 | tf_op jit(solution)/shard_map/ppermute | solution.py:30
  120.6 4.6 %collective-permute-done.4 = bf16[3456,384]{1,0:T(8,128)(2,1)} collective-permute-done((bf16[3456,384]{1,0:T(8,128)(2,1)}, bf16[3456,384]{1,0:T(8,128)(2,1)}, u32[]{:S(2)}, u32[]{:S(2)}) %collective-permute-start.4) | collective-permute-done | bytes 2654240 | tf_op jit(solution)/shard_map/ppermute | solution.py:30
  125.2 9.3 %fusion.25 = f32[1536,384]{1,0:T(8,128)S(1)} fusion(bf16[1536,3456]{1,0:T(8,128)(2,1)} %bitcast.7, bf16[3456,384]{1,0:T(8,128)(2,1)} %bitcast.6, bf16[3456,384]{1,0:T(8,128)(2,1)} %collective-permute-done.4, pred[]{:T(512)S(6)} %eq.50), kind=kOutput, calls=%fused_computation.37 | convolution fusion | flops 4078190592 | bytes 18284544 | tf_op jit(solution)/shard_map/dot_general | solution.py:99
  135.7 6.3 %fusion.47 = bf16[32,48,384]{2,1,0:T(8,128)(2,1)S(1)} fusion(bf16[32,48,384]{2,1,0:T(8,128)(2,1)S(1)} %get-tuple-element.12, f32[384]{0:T(512)S(1)} %get-tuple-element.24, f32[32,48]{1,0:T(8,128)S(1)} %add_rsqrt_fusion.1, f32[32,48]{1,0:T(8,128)S(1)} %broadcast_multiply_fusion.1, pred[32,48]{1,0:T(8,128)(4,1)S(1)} %and_and_fusion), kind=kLoop, calls=%fused_computation.69 | loop fusion | flops 41287680 | bytes 2374656 | tf_op jit(solution)/shard_map/jit(_where)/select_n | solution.py:116
  142.6 3.9 %broadcast_select_fusion = (bf16[16,32,384]{2,1,0:T(8,128)(2,1)S(1)}, bf16[16,32,384]{2,1,0:T(8,128)(2,1)S(1)}, bf16[1,1,16,32,384]{4,3,2,1,0:T(8,128)(2,1)S(1)}) fusion(pred[]{:T(512)S(6)} %eq.50, bf16[32,48,384]{2,1,0:T(8,128)(2,1)S(1)} %get-tuple-element.12, bf16[16,32,3456]{2,1,0:T(8,128)(2,1)S(1)} %slice_dynamic-update-slice_fusion.9, ...), kind=kOutput, calls=%fused_computation.100 | convolution fusion | flops 1361068032 | bytes 10421248 | tf_op jit(solution)/shard_map/dot_general | solution.py:118
  150.0 17.7 %all_to_all.25 = bf16[32,13,256]{2,1,0:T(8,128)(2,1)S(1)} all-to-all(bf16[32,13,256]{2,1,0:T(8,128)(2,1)S(1)} %copy.42), channel_id=1, replica_groups=mesh['section'=2,'sy'=8,'sx'=8,'mb'=4] {'sx','mb'}, dimensions={0} | all-to-all | bytes 425984 | tf_op jit(solution)/shard_map/all_to_all | solution.py:151
  170.3 4.8 %all-to-all-start.3 = ((bf16[16,13,256]{2,1,0:T(8,128)(2,1)}), bf16[16,13,256]{2,1,0:T(8,128)(2,1)S(1)}, u32[]{:S(2)}, u32[]{:S(2)}) async-start(bf16[16,13,256]{2,1,0:T(8,128)(2,1)} %broadcast_in_dim.75), calls=%async_computation.3 | async-start | bytes 262144 | tf_op jit(solution)/shard_map/all_to_all | solution.py:20
  175.2 2.1 %collective-permute-start.5 = (bf16[16,32,384]{2,1,0:T(8,128)(2,1)S(1)}, bf16[16,32,384]{2,1,0:T(8,128)(2,1)S(1)}, u32[]{:S(2)}, u32[]{:S(2)}) collective-permute-start(bf16[16,32,384]{2,1,0:T(8,128)(2,1)S(1)} %get-tuple-element.9), channel_id=1, source_target_pairs={{0,256},{256,0},{1,257},{257,1},{2,258},{258,2},{3,259},{259,3},{4... | collective-permute-start | bytes 1179656 | tf_op jit(solution)/shard_map/ppermute | solution.py:30
  177.3 6.2 %all-to-all-done.3 = bf16[16,13,256]{2,1,0:T(8,128)(2,1)S(1)} async-done(((bf16[16,13,256]{2,1,0:T(8,128)(2,1)}), bf16[16,13,256]{2,1,0:T(8,128)(2,1)S(1)}, u32[]{:S(2)}, u32[]{:S(2)}) %all-to-all-start.3) | async-done | bytes 106528 | tf_op jit(solution)/shard_map/all_to_all | solution.py:20
  184.2 3.9 %all-to-all-start.4 = ((bf16[32,12,256]{2,1,0:T(8,128)(2,1)}), bf16[32,12,256]{2,1,0:T(8,128)(2,1)S(1)}, u32[]{:S(2)}, u32[]{:S(2)}) async-start(bf16[32,12,256]{2,1,0:T(8,128)(2,1)} %broadcast_in_dim.76), calls=%async_computation.4 | async-start | bytes 524288 | tf_op jit(solution)/shard_map/all_to_all | solution.py:20
  191.0 10.0 %all-to-all-done.4 = bf16[32,12,256]{2,1,0:T(8,128)(2,1)S(1)} async-done(((bf16[32,12,256]{2,1,0:T(8,128)(2,1)}), bf16[32,12,256]{2,1,0:T(8,128)(2,1)S(1)}, u32[]{:S(2)}, u32[]{:S(2)}) %all-to-all-start.4) | async-done | bytes 196640 | tf_op jit(solution)/shard_map/all_to_all | solution.py:20
  (73 shorter events, 13.7 us)
Async XLA Ops:
  0.6 119.5 %copy-start = (bf16[1,32,32,256]{3,2,1,0:T(8,128)(2,1)S(1)}, bf16[1,32,32,256]{3,2,1,0:T(8,128)(2,1)}, u32[]{:S(2)}) copy-start(bf16[1,32,32,256]{3,2,1,0:T(8,128)(2,1)} %param.12) | copy-start | bytes 1572868
  2.8 14.1 %copy-start.5 = (f32[1,1,384]{2,1,0:T(1,128)S(1)}, f32[1,1,384]{2,1,0:T(1,128)}, u32[]{:S(2)}) copy-start(f32[1,1,384]{2,1,0:T(1,128)} %param.10) | copy-start | bytes 4612
  2.8 16.1 %copy-start.3 = (bf16[1,1,54,384]{3,2,1,0:T(8,128)(2,1)S(1)}, bf16[1,1,54,384]{3,2,1,0:T(8,128)(2,1)}, u32[]{:S(2)}) copy-start(bf16[1,1,54,384]{3,2,1,0:T(8,128)(2,1)} %param.9) | copy-start | bytes 124420
  2.8 11.1 %collective-permute-start = (bf16[9,32,384]{2,1,0:T(8,128)(2,1)S(1)}, bf16[9,32,384]{2,1,0:T(8,128)(2,1)S(1)}, u32[]{:S(2)}, u32[]{:S(2)}) collective-permute-start(bf16[9,32,384]{2,1,0:T(8,128)(2,1)S(1)} %slice_select_fusion), channel_id=1, source_target_pairs={{0,32},{32,64},{64,96},{96,128},{128,160},{160,192},{192,224},{288... | collective-permute-start | bytes 663560 | tf_op jit(solution)/shard_map/ppermute | solution.py:81
  14.2 16.9 %collective-permute-start.1 = (bf16[34,9,384]{2,1,0:T(8,128)(2,1)S(1)}, bf16[34,9,384]{2,1,0:T(8,128)(2,1)S(1)}, u32[]{:S(2)}, u32[]{:S(2)}) collective-permute-start(bf16[34,9,384]{2,1,0:T(8,128)(2,1)S(1)} %get-tuple-element.16), channel_id=1, source_target_pairs={{0,4},{4,8},{8,12},{12,16},{16,20},{20,24},{24,28},{1,5},{5,9},{9,... | collective-permute-start | bytes 705032 | tf_op jit(solution)/shard_map/ppermute | solution.py:89
  15.6 16.4 %collective-permute-start.2 = (bf16[34,9,384]{2,1,0:T(8,128)(2,1)S(1)}, bf16[34,9,384]{2,1,0:T(8,128)(2,1)}, u32[]{:S(2)}, u32[]{:S(2)}) collective-permute-start(bf16[34,9,384]{2,1,0:T(8,128)(2,1)S(1)} %get-tuple-element.17), channel_id=1, source_target_pairs={{4,0},{8,4},{12,8},{16,12},{20,16},{24,20},{28,24},{5,1},{9,5},{13... | collective-permute-start | bytes 705032 | tf_op jit(solution)/shard_map/ppermute | solution.py:90
  16.9 14.3 %collective-permute-start.3 = (f32[384]{0:T(512)S(1)}, f32[384]{0:T(512)S(1)}, u32[]{:S(2)}, u32[]{:S(2)}) collective-permute-start(f32[384]{0:T(512)S(1)} %reduce.1), channel_id=1, source_target_pairs={{0,256},{256,0},{1,257},{257,1},{2,258},{258,2},{3,259},{259,3},{4... | collective-permute-start | bytes 4616 | tf_op jit(solution)/shard_map/ppermute | solution.py:30
  19.6 25.8 %all-to-all-start = ((bf16[8,54,384]{2,1,0:T(8,128)(2,1)}), bf16[8,54,384]{2,1,0:T(8,128)(2,1)S(1)}, u32[]{:S(2)}, u32[]{:S(2)}) async-start(bf16[8,54,384]{2,1,0:T(8,128)(2,1)} %broadcast_in_dim.65), calls=%async_computation | async-start | bytes 688128 | tf_op jit(solution)/shard_map/all_to_all | solution.py:20
  31.2 0.8 copy-start.1
  47.2 70.7 %all-to-all-start.1 = ((bf16[8,432,384]{2,1,0:T(8,128)(2,1)}), bf16[8,432,384]{2,1,0:T(8,128)(2,1)}, u32[]{:S(2)}, u32[]{:S(2)}) async-start(bf16[8,432,384]{2,1,0:T(8,128)(2,1)} %stack.3), calls=%async_computation.1 | async-start | bytes 5308416 | tf_op jit(solution)/shard_map/all_to_all | solution.py:67
  74.5 45.9 %copy-start.4 = (s32[1,32,32]{2,1,0:T(8,128)S(1)}, s32[1,32,32]{2,1,0:T(8,128)}, u32[]{:S(2)}) copy-start(s32[1,32,32]{2,1,0:T(8,128)} %param.13) | copy-start | bytes 12292
  118.0 7.2 %collective-permute-start.4 = (bf16[3456,384]{1,0:T(8,128)(2,1)}, bf16[3456,384]{1,0:T(8,128)(2,1)}, u32[]{:S(2)}, u32[]{:S(2)}) collective-permute-start(bf16[3456,384]{1,0:T(8,128)(2,1)} %bitcast.6), channel_id=1, source_target_pairs={{0,256},{256,0},{1,257},{257,1},{2,258},{258,2},{3,259},{259,3},{4... | collective-permute-start | bytes 7962632 | tf_op jit(solution)/shard_map/ppermute | solution.py:30
  142.6 4.2 %copy-start.2 = (bf16[384,256]{1,0:T(8,128)(2,1)S(1)}, bf16[384,256]{1,0:T(8,128)(2,1)}, u32[]{:S(2)}) copy-start(bf16[384,256]{1,0:T(8,128)(2,1)} %param.11) | copy-start | bytes 589828
  170.3 13.1 %all-to-all-start.3 = ((bf16[16,13,256]{2,1,0:T(8,128)(2,1)}), bf16[16,13,256]{2,1,0:T(8,128)(2,1)S(1)}, u32[]{:S(2)}, u32[]{:S(2)}) async-start(bf16[16,13,256]{2,1,0:T(8,128)(2,1)} %broadcast_in_dim.75), calls=%async_computation.3 | async-start | bytes 262144 | tf_op jit(solution)/shard_map/all_to_all | solution.py:20
  175.2 12.9 %collective-permute-start.5 = (bf16[16,32,384]{2,1,0:T(8,128)(2,1)S(1)}, bf16[16,32,384]{2,1,0:T(8,128)(2,1)S(1)}, u32[]{:S(2)}, u32[]{:S(2)}) collective-permute-start(bf16[16,32,384]{2,1,0:T(8,128)(2,1)S(1)} %get-tuple-element.9), channel_id=1, source_target_pairs={{0,256},{256,0},{1,257},{257,1},{2,258},{258,2},{3,259},{259,3},{4... | collective-permute-start | bytes 1179656 | tf_op jit(solution)/shard_map/ppermute | solution.py:30
  184.2 16.8 %all-to-all-start.4 = ((bf16[32,12,256]{2,1,0:T(8,128)(2,1)}), bf16[32,12,256]{2,1,0:T(8,128)(2,1)S(1)}, u32[]{:S(2)}, u32[]{:S(2)}) async-start(bf16[32,12,256]{2,1,0:T(8,128)(2,1)} %broadcast_in_dim.76), calls=%async_computation.4 | async-start | bytes 524288 | tf_op jit(solution)/shard_map/all_to_all | solution.py:20
